TPU v7x, 32 devices: a whole 2x2x4 slice. The times are simulated.
32 devices in a mesh: gx: 8 (over y, x, core), gy: 4 (over z).
Axes of the slice: x: 2, y: 2, z: 4, core: 2. Of those that a mesh axis runs over, the one named last changes fastest.
Arguments:
- support_funcs: bfloat16 [3072, 16, 128], P('gx', 'gy'), may hold values from -6 to 6
- potential: float32 [16, 128], P('gy'), may hold values from -1 to 1
- kernel: bfloat16 [4, 48, 64, 64], P('gy', 'gx'), may hold values from -0.375 to 0.375
- weighted: bfloat16 [4, 48, 64, 64], P('gy', 'gx'), may hold values from -0.375 to 0.375
- columns: int32 [48, 4], P('gx'), may hold values from 0 to 47, as said below
- regions: int32 [48, 4], P('gx'), may hold values from 0 to 128, as said below
Outputs:
- new_support: float32 [3072, 16, 128], P('gx', 'gy')
- hamiltonian: float32 [4, 48, 64, 64], P('gy', 'gx')
Inputs may be any that keep to these rules, and one draw needn't show every extreme that they name: `columns`: the column blocks of row block a are 4 distinct blocks among the 18 blocks owned by gx index a // 6 and its two neighbours, counted cyclically. `regions`: every box spans at least half of 16 along y and half of 128 along z; it starts at 0 in both dimensions where the block index is even and ends at 16 and 128 where it is odd.
All inputs are finite; a program needn't handle non-finite values.
Results may differ from a plain program's by a relative error of at most 0.0011.
Values may be sent and summed in bfloat16 or wider, within the bound.
A program may use at most 64 MiB of HBM per device.

v0:
```python
import functools

import jax
import jax.numpy as jnp
from jax import lax
from jax.experimental import pallas as pl
from jax.experimental.pallas import tpu as pltpu
from jax.sharding import PartitionSpec as P

SWEEPS = 3
CHUNK = 2
kinetic_cut = 1.0
step_length = 0.5
f32 = jnp.float32
bf16 = jnp.bfloat16


def remote(src, dst, send, recv, **device):
    return pltpu.make_async_remote_copy(
        src_ref=src,
        dst_ref=dst,
        send_sem=send,
        recv_sem=recv,
        device_id=device,
        device_id_type=pl.DeviceIdType.MESH,
    )


def unrolled(count, body):
    for i in range(count):
        body(i)


def loop(count, body):
    def step(i, carry):
        body(i)
        return carry

    lax.fori_loop(0, count, step, 0)


def kernel_body(
    n_gx, n_gy, rows_y,
    cols_hbm, regs_hbm, pot_hbm, x_hbm, kern_hbm, wght_hbm,
    out_ref, ham_ref,
    cols_ref, regs_ref, pot_ref, x_ref, kern_ref, wght_ref, raw, wide, near_phi, near_app, edge_send, edge_recv, pack, packs,
    grad, halo_send, halo_recv, part, part_half, part_recv, half_recv, in_sem,
    x_send, x_recv, e_send, e_recv, k_send, k_recv, k_own, g_send, g_recv, h_send, h_recv, b_send, b_recv,
):
    gx, gy = lax.axis_index("gx"), lax.axis_index("gy")
    right, left = lax.rem(gx + 1, n_gx), lax.rem(gx + n_gx - 1, n_gx)
    own_slots, nb, size = kern_ref.shape[:3]
    slots = own_slots * n_gy
    depth = x_ref.shape[1]
    brick = size * rows_y
    chunks = nb // CHUNK
    rows = CHUNK * brick
    half = size // 2
    has_low, has_high = gy > 0, gy < n_gy - 1
    volume = 1.0 / (rows_y * n_gy * depth)

    pairs = (
        (x_hbm, x_ref), (kern_hbm, kern_ref), (wght_hbm, wght_ref),
        (pot_hbm, pot_ref), (cols_hbm, cols_ref), (regs_hbm, regs_ref),
    )
    loads = [pltpu.make_async_copy(src, dst, in_sem.at[i]) for i, (src, dst) in enumerate(pairs)]
    for load in loads:
        load.start()
    barrier = pltpu.get_barrier_semaphore()
    for device in (left, right):
        pl.semaphore_signal(barrier, device_id={"gx": device}, device_id_type=pl.DeviceIdType.MESH)
    for off in range(1, n_gy):
        pl.semaphore_signal(
            barrier, device_id={"gy": lax.rem(gy + off, n_gy)}, device_id_type=pl.DeviceIdType.MESH
        )
    loads[1].wait()
    loads[2].wait()
    for j in range(own_slots):
        for a in range(nb):
            pack[j, a] = jnp.concatenate([kern_ref[j, a], wght_ref[j, a]], axis=1)
    pl.semaphore_wait(barrier, 2 + n_gy - 1)

    def x_copy(to_right, c):
        piece = pl.ds(pl.multiple_of(c * rows, rows), rows)
        group = 0 if to_right else 2
        return remote(
            x_hbm.at[piece], raw.at[group, piece], x_send.at[group, c], x_recv.at[group, c],
            gx=right if to_right else left,
        )

    def start_x(c):
        x_copy(True, c).start()
        x_copy(False, c).start()

    unrolled(chunks, start_x)

    def k_copy(up, d):
        origin = gy - (d - 1) if up else gy + (d - 1)
        place = pl.ds(jnp.clip(origin, 0, n_gy - 1) * own_slots, own_slots)
        side = 0 if up else 1
        return remote(
            pack if d == 1 else packs.at[place], packs.at[place],
            k_send.at[side, d - 1], k_recv.at[side, d - 1],
            gy=jnp.minimum(gy + 1, n_gy - 1) if up else jnp.maximum(gy - 1, 0),
        )

    def k_sends(d, action):
        pl.when((gy - (d - 1) >= 0) & has_high)(lambda: action(k_copy(True, d)))
        pl.when((gy + (d - 1) < n_gy) & has_low)(lambda: action(k_copy(False, d)))

    def k_arrived(d):
        pl.when(gy - d >= 0)(lambda: k_copy(True, d).wait_recv())
        pl.when(gy + d < n_gy)(lambda: k_copy(False, d).wait_recv())

    def k_relay(d):
        k_arrived(d - 1)
        k_sends(d, lambda copy: copy.start())

    own_copy = pltpu.make_async_copy(pack, packs.at[pl.ds(gy * own_slots, own_slots)], k_own)
    own_copy.start()

    def base_of(p):
        if isinstance(p, int):
            return p * brick
        return pl.multiple_of(p * brick, brick)

    def spread(group, c, source):
        for i in range(CHUNK):
            b = c * CHUNK + i
            p = group * nb + b
            wide[pl.ds(base_of(p), brick), :] = source(b).astype(f32)
            for y in range(rows_y):
                row = wide[pl.ds(base_of(p) + y, size, stride=rows_y), :].astype(bf16)
                near_phi[p, :, y * depth : (y + 1) * depth] = row
                if y == 0:
                    edge_send[0, p] = row
                if y == rows_y - 1:
                    edge_send[1, p] = row

    def edge_copy(side, group, c):
        piece = pl.ds(group * nb + c * CHUNK, CHUNK)
        index = group * chunks + c
        return remote(
            edge_send.at[side, piece], edge_recv.at[1 - side, piece],
            e_send.at[side, index], e_recv.at[1 - side, index],
            gy=jnp.maximum(gy - 1, 0) if side == 0 else jnp.minimum(gy + 1, n_gy - 1),
        )

    def both_sides(action):
        pl.when(has_low)(lambda: action(0))
        pl.when(has_high)(lambda: action(1))

    def own_chunk(c):
        spread(1, c, lambda b: x_ref[pl.ds(pl.multiple_of(b * brick, brick), brick), :])
        both_sides(lambda side: edge_copy(side, 1, c).start())

    def far_chunk(group, c):
        piece = pl.ds(pl.multiple_of(c * rows, rows), rows)
        remote(
            x_hbm.at[piece], raw.at[group, piece], x_send.at[group, c], x_recv.at[group, c], gx=right
        ).wait_recv()
        spread(group, c, lambda b: raw[group, pl.ds(pl.multiple_of(b * brick, brick), brick), :])
        both_sides(lambda side: edge_copy(side, group, c).start())

    def apply_chunk(group, c):
        pl.when(has_low)(lambda: edge_copy(1, group, c).wait_recv())
        pl.when(has_high)(lambda: edge_copy(0, group, c).wait_recv())
        for i in range(CHUNK):
            p = group * nb + c * CHUNK + i
            line = [edge_recv[0, p].astype(f32)]
            line += [
                near_phi[p, :, y * depth : (y + 1) * depth].astype(f32) for y in range(rows_y)
            ]
            line += [edge_recv[1, p].astype(f32)]
            for y in range(rows_y):
                center = line[y + 1]
                beside = (
                    line[y + 2] + line[y] + pltpu.roll(center, 1, 1) + pltpu.roll(center, depth - 1, 1)
                )
                applied = -0.5 * (beside - 4.0 * center) + pot_ref[y : y + 1, :] * center
                near_app[p, :, y * depth : (y + 1) * depth] = applied.astype(bf16)

    @pl.when(gy == 0)
    def _():
        edge_recv[0] = jnp.zeros(edge_recv.shape[1:], bf16)
        halo_recv[0] = jnp.zeros(halo_recv.shape[1:], bf16)

    @pl.when(gy == n_gy - 1)
    def _():
        edge_recv[1] = jnp.zeros(edge_recv.shape[1:], bf16)
        halo_recv[1] = jnp.zeros(halo_recv.shape[1:], bf16)

    first = 2 - 2 * lax.rem(gx, 2)
    second = 2 - first
    loads[0].wait()
    unrolled(chunks, own_chunk)
    k_sends(1, lambda copy: copy.start())
    for load in loads[3:]:
        load.wait()
    unrolled(chunks, lambda c: far_chunk(first, c))
    if n_gy > 2:
        k_relay(2)
    unrolled(chunks, lambda c: apply_chunk(1, c))
    for d in range(3, n_gy):
        k_relay(d)
    own_copy.wait()

    def interleaved(c):
        far_chunk(second, c)
        apply_chunk(first, c)

    unrolled(chunks, interleaved)
    unrolled(chunks, lambda c: apply_chunk(second, c))
    k_arrived(n_gy - 1)

    def picks(a):
        start = nb * n_gx + nb - nb * gx
        found = [lax.rem(cols_ref[k, a] + start, nb * n_gx) for k in range(slots)]
        return [jnp.minimum(p, 3 * nb - 1) for p in found]

    def halo_copy(side, a):
        return remote(
            halo_send.at[side, a], halo_recv.at[1 - side, a], g_send.at[side, a], g_recv.at[1 - side, a],
            gy=jnp.maximum(gy - 1, 0) if side == 0 else jnp.minimum(gy + 1, n_gy - 1),
        )

    def gradient_of(a):
        where = picks(a)
        blocks = [packs[k, a] for k in range(slots)]
        mixing = jnp.concatenate(
            [b[:, :size] for b in blocks] + [-b[:, size:] for b in blocks], axis=1
        )
        source = jnp.concatenate([near_app[p] for p in where] + [near_phi[p] for p in where], axis=0)
        total = jnp.dot(mixing, source, preferred_element_type=f32)
        for y in range(rows_y):
            piece = total[:, y * depth : (y + 1) * depth]
            grad[a, y] = piece
            if y < SWEEPS:
                halo_send[0, a, y] = piece.astype(bf16)
            if y >= rows_y - SWEEPS:
                halo_send[1, a, y - rows_y + SWEEPS] = piece.astype(bf16)
        both_sides(lambda side: halo_copy(side, a).start())

    unrolled(nb, gradient_of)

    def part_of(a):
        source = jnp.concatenate([near_app[p] for p in picks(a)], axis=0)
        block = lax.dot_general(
            near_phi[nb + a], source, (((1,), (1,)), ((), ())), preferred_element_type=f32
        ) * volume
        for k in range(slots):
            one = block[:, k * size : (k + 1) * size]
            one = jnp.concatenate([one[:half], one[half:]], axis=1)
            part[k, a] = one
            part_half[k, a] = one.astype(bf16)

    unrolled(nb, part_of)

    def part_copy(off, wide_type):
        peer = lax.rem(gy + off, n_gy)
        source, target = (part, part_recv) if wide_type else (part_half, half_recv)
        send, recv = (h_send, h_recv) if wide_type else (b_send, b_recv)
        return remote(
            source.at[pl.ds(peer * own_slots, own_slots)], target.at[off - 1],
            send.at[off - 1], recv.at[off - 1], gy=peer,
        )

    def by_distance(off, other, action):
        apart = jnp.abs(other - gy)
        pl.when(apart == 1)(lambda: action(off, True))
        pl.when(apart > 1)(lambda: action(off, False))

    for off in range(1, n_gy):
        by_distance(off, lax.rem(gy + off, n_gy), lambda o, w: part_copy(o, w).start())

    diag = 1.0 + 2.0 / kinetic_cut
    coef = 0.5 / kinetic_cut
    low, high = jnp.where(has_low, 1.0, 0.0).astype(f32), jnp.where(has_high, 1.0, 0.0).astype(f32)
    z_index = lax.broadcasted_iota(jnp.int32, (size, depth), 1)

    def finish(a):
        pl.when(has_low)(lambda: halo_copy(1, a).wait_recv())
        pl.when(has_high)(lambda: halo_copy(0, a).wait_recv())
        field = [halo_recv[0, a, i].astype(f32) for i in range(SWEEPS)]
        field += [grad[a, y] for y in range(rows_y)]
        field += [halo_recv[1, a, i].astype(f32) for i in range(SWEEPS)]
        field = [value * (1.0 / diag) for value in field]
        now = list(field)
        for sweep in range(1, SWEEPS + 1):
            later = list(now)
            for i in range(sweep, rows_y + 2 * SWEEPS - sweep):
                beside = now[i - 1] + now[i + 1]
                beside = beside + pltpu.roll(now[i], 1, 1) + pltpu.roll(now[i], depth - 1, 1)
                value = field[i] + (coef / diag) * beside
                if i < SWEEPS:
                    value = value * low
                if i >= rows_y + SWEEPS:
                    value = value * high
                later[i] = value
            now = later
        z_in = (z_index >= regs_ref[2, a]) & (z_index < regs_ref[3, a])
        for y in range(rows_y):
            spot = gy * rows_y + y
            y_in = jnp.where((spot >= regs_ref[0, a]) & (spot < regs_ref[1, a]), step_length, 0.0)
            masked = jnp.where(z_in, now[SWEEPS + y] * y_in.astype(f32), 0.0)
            phi = near_phi[nb + a, :, y * depth : (y + 1) * depth].astype(f32)
            out_ref[pl.ds(a * brick + y, size, stride=rows_y), :] = phi - masked

    unrolled(nb, finish)

    mine = pl.ds(gy * own_slots, own_slots)

    def take(off, wide_type):
        part_copy(off, wide_type).wait_recv()
        part[mine] = part[mine] + (part_recv if wide_type else half_recv)[off - 1].astype(f32)

    for off in range(1, n_gy):
        by_distance(off, lax.rem(gy + n_gy - off, n_gy), take)
    for j in range(own_slots):
        for a in range(nb):
            total = part[gy * own_slots + j, a]
            ham_ref[j, a, :half, :] = total[:, :size]
            ham_ref[j, a, half:, :] = total[:, size:]

    def sent_x(c):
        x_copy(True, c).wait_send()
        x_copy(False, c).wait_send()

    loop(chunks, sent_x)
    for group in range(3):
        loop(chunks, lambda c: both_sides(lambda side: edge_copy(side, group, c).wait_send()))
    loop(nb, lambda a: both_sides(lambda side: halo_copy(side, a).wait_send()))
    for off in range(1, n_gy):
        k_sends(off, lambda copy: copy.wait_send())
        by_distance(off, lax.rem(gy + off, n_gy), lambda o, w: part_copy(o, w).wait_send())


def store_body(support_ref, ham_ref, support_out, ham_out, sem):
    copies = [
        pltpu.make_async_copy(support_ref, support_out, sem.at[0]),
        pltpu.make_async_copy(ham_ref, ham_out, sem.at[1]),
    ]
    for copy in copies:
        copy.start()
    for copy in copies:
        copy.wait()


def local(n_gx, n_gy, support_funcs, potential, kernel, weighted, columns, regions):
    own_slots, nb, size = kernel.shape[:3]
    orbitals, rows_y, depth = support_funcs.shape
    slots = own_slots * n_gy
    flat = orbitals * rows_y
    chunks = nb // CHUNK
    vmem = pl.BlockSpec(memory_space=pltpu.VMEM)
    dma = pltpu.SemaphoreType.DMA
    operands = (
        columns.T, regions.T, potential, support_funcs.reshape(flat, depth), kernel, weighted
    )
    new_support, hamiltonian = pl.pallas_call(
        functools.partial(kernel_body, n_gx, n_gy, rows_y),
        out_shape=(
            jax.ShapeDtypeStruct((flat, depth), f32),
            jax.ShapeDtypeStruct((own_slots, nb, size, size), f32),
        ),
        in_specs=[pl.BlockSpec(memory_space=pltpu.HBM)] * 6,
        out_specs=(vmem, vmem),
        scratch_shapes=[
            pltpu.SMEM((slots, nb), jnp.int32),
            pltpu.SMEM((4, nb), jnp.int32),
            pltpu.VMEM((rows_y, depth), f32),
            pltpu.VMEM((flat, depth), bf16),
            pltpu.VMEM(kernel.shape, bf16),
            pltpu.VMEM(kernel.shape, bf16),
            pltpu.VMEM((3, flat, depth), bf16),
            pltpu.VMEM((3 * flat, depth), f32),
            pltpu.VMEM((3 * nb, size, rows_y * depth), bf16),
            pltpu.VMEM((3 * nb, size, rows_y * depth), bf16),
            pltpu.VMEM((2, 3 * nb, size, depth), bf16),
            pltpu.VMEM((2, 3 * nb, size, depth), bf16),
            pltpu.VMEM((own_slots, nb, size, 2 * size), bf16),
            pltpu.VMEM((slots, nb, size, 2 * size), bf16),
            pltpu.VMEM((nb, rows_y, size, depth), f32),
            pltpu.VMEM((2, nb, SWEEPS, size, depth), bf16),
            pltpu.VMEM((2, nb, SWEEPS, size, depth), bf16),
            pltpu.VMEM((slots, nb, size // 2, 2 * size), f32),
            pltpu.VMEM((slots, nb, size // 2, 2 * size), bf16),
            pltpu.VMEM((n_gy - 1, own_slots, nb, size // 2, 2 * size), f32),
            pltpu.VMEM((n_gy - 1, own_slots, nb, size // 2, 2 * size), bf16),
            dma((6,)),
            dma((3, chunks)),
            dma((3, chunks)),
            dma((2, 3 * chunks)),
            dma((2, 3 * chunks)),
            dma((2, n_gy - 1)),
            dma((2, n_gy - 1)),
            dma(()),
            dma((2, nb)),
            dma((2, nb)),
            dma((n_gy - 1,)),
            dma((n_gy - 1,)),
            dma((n_gy - 1,)),
            dma((n_gy - 1,)),
        ],
        compiler_params=pltpu.CompilerParams(
            collective_id=0, has_side_effects=True, vmem_limit_bytes=40 * 1024 * 1024
        ),
    )(*[pltpu.with_memory_space_constraint(v, pltpu.HBM) for v in operands])
    hbm = pl.BlockSpec(memory_space=pltpu.HBM)
    new_support, hamiltonian = pl.pallas_call(
        store_body,
        out_shape=(
            jax.ShapeDtypeStruct(new_support.shape, f32),
            jax.ShapeDtypeStruct(hamiltonian.shape, f32),
        ),
        in_specs=[vmem, vmem],
        out_specs=(hbm, hbm),
        scratch_shapes=[dma((2,))],
        compiler_params=pltpu.CompilerParams(vmem_limit_bytes=8 * 1024 * 1024),
    )(new_support, hamiltonian)
    return (new_support.reshape(orbitals, rows_y, depth), hamiltonian)


def solution(mesh):
    return jax.shard_map(
        functools.partial(local, mesh.shape["gx"], mesh.shape["gy"]),
        mesh=mesh,
        in_specs=(
            P("gx", "gy", None),
            P("gy", None),
            P("gy", "gx", None, None),
            P("gy", "gx", None, None),
            P("gx", None),
            P("gx", None),
        ),
        out_specs=(P("gx", "gy", None), P("gy", "gx", None, None)),
        check_vma=False,
    )
```

profile of v0, /device:TPU:0, one launch (start us, length us, event | category | flops | bytes accessed | tf_op | source)
XLA Modules:
  0.0 34.0 jit_solution(4202141020311319450)
XLA Ops:
  0.6 32.4 %shard_map.77 = (f32[1536,128]{1,0:T(8,128)S(1)}, f32[1,6,64,64]{3,2,1,0:T(8,128)S(1)}) custom-call(s32[4,6]{1,0:T(4,128)} %bitcast.5, s32[4,6]{1,0:T(4,128)} %bitcast.6, f32[4,128]{1,0:T(4,128)} %pot_hbm.1, bf16[1536,128]{1,0:T(8,128)(2,1)} %bitcast.4, bf16[1,6,64,64]{3,2,1,0:T(8,128)(2,1)} %kern_hbm.1, bf16[1,6,64,64]{3,2,1,0:T(8,128)(2,1)} %wght_hbm.1), custom_call_target="tpu_custom_call" | custom-call | tf_op jit(solution)/shard_map/pallas_call | solution.py:360
  33.1 1.0 %shard_map.78 = (f32[1536,128]{1,0:T(8,128)}, f32[1,6,64,64]{3,2,1,0:T(8,128)}) custom-call(f32[1536,128]{1,0:T(8,128)S(1)} %get-tuple-element.6.support_ref, f32[1,6,64,64]{3,2,1,0:T(8,128)S(1)} %get-tuple-element.7.ham_ref), custom_call_target="tpu_custom_call" | custom-call | tf_op jit(solution)/shard_map/pallas_call | solution.py:410
where the time goes:
time: 34.2 us; the launch traced here: 34 us
  Pallas kernels  33.4 us (98%)
  between operations  0.64 us (2%)
    pallas_call x1, Pallas kernels, local(): pl.pallas_call(functools.partial(kernel_body, n_gx, n_gy, rows_y), out_sh...  32.4 us
    pallas_call x1, Pallas kernels, local(): pl.pallas_call(store_body, out_shape=(jax.ShapeDtypeStruct(new_support.sh...  0.96 us

commit v1 on v0

v1 whole, which is shorter than its diff:
```python
import functools

import jax
import jax.numpy as jnp
from jax import lax
from jax.experimental import pallas as pl
from jax.experimental.pallas import tpu as pltpu
from jax.sharding import PartitionSpec as P

SWEEPS = 3
CHUNK = 2
HALVES = 2
TOP = 32767.0
kinetic_cut = 1.0
step_length = 0.5
f32 = jnp.float32
bf16 = jnp.bfloat16


def remote(src, dst, send, recv, **device):
    return pltpu.make_async_remote_copy(
        src_ref=src,
        dst_ref=dst,
        send_sem=send,
        recv_sem=recv,
        device_id=device,
        device_id_type=pl.DeviceIdType.MESH,
    )


def signal(barrier, **device):
    pl.semaphore_signal(barrier, device_id=device, device_id_type=pl.DeviceIdType.MESH)


def kernel_body(
    n_gx, n_gy, rows_y,
    cols_hbm, regs_hbm, pot_hbm, x_hbm, kern_hbm, wght_hbm,
    out_ref, ham_ref,
    cols_ref, regs_ref, pot_ref, x_ref, kern_ref, wght_ref, wide, phi, app, edges, packs,
    grad, halo_out, halo_in, part, code_out, code_in, top_out, top_in, in_sem,
    x_send, x_recv, e_send, e_recv, f_send, f_recv, k_send, k_recv, g_send, g_recv,
    h_send, h_recv, t_send, t_recv,
):
    gx, gy = lax.axis_index("gx"), lax.axis_index("gy")
    right, left = lax.rem(gx + 1, n_gx), lax.rem(gx + n_gx - 1, n_gx)
    partner = gx + 1 - 2 * lax.rem(gx, 2)
    above, below = jnp.minimum(gy + 1, n_gy - 1), jnp.maximum(gy - 1, 0)
    has_low, has_high = gy > 0, gy < n_gy - 1
    near = 2 - 2 * lax.rem(gx, 2)
    far = 2 - near
    own_slots, nb, size = kern_ref.shape[:3]
    slots = own_slots * n_gy
    depth = x_ref.shape[1]
    brick = size * rows_y
    chunks = nb // CHUNK
    half = size // 2
    volume = 1.0 / (rows_y * n_gy * depth)
    inner, outer = tuple(range(1, rows_y - 1)), (0, rows_y - 1)

    pairs = (
        (x_hbm, x_ref), (kern_hbm, kern_ref), (wght_hbm, wght_ref),
        (pot_hbm, pot_ref), (cols_hbm, cols_ref), (regs_hbm, regs_ref),
    )
    loads = [pltpu.make_async_copy(src, dst, in_sem.at[i]) for i, (src, dst) in enumerate(pairs)]
    for load in loads:
        load.start()
    barrier = pltpu.get_barrier_semaphore()
    signal(barrier, gx=left)
    signal(barrier, gx=right)
    pl.when(has_low)(lambda: signal(barrier, gy=below))
    pl.when(has_high)(lambda: signal(barrier, gy=above))

    def both_sides(action):
        pl.when(has_low)(lambda: action(0))
        pl.when(has_high)(lambda: action(1))

    def beside(side):
        return below if side == 0 else above

    @pl.when(gy == 0)
    def _():
        edges[0] = jnp.zeros(edges.shape[1:], bf16)
        halo_in[0] = jnp.zeros(halo_in.shape[1:], bf16)

    @pl.when(gy == n_gy - 1)
    def _():
        edges[1] = jnp.zeros(edges.shape[1:], bf16)
        halo_in[1] = jnp.zeros(halo_in.shape[1:], bf16)

    def group_at(group):
        return pl.ds(group * nb, nb)

    def x_copy(group, y):
        return remote(
            phi.at[y, group_at(1)], phi.at[y, group_at(group)],
            x_send.at[group, y], x_recv.at[group, y], gx=right if isinstance(group, int) and group == 0 else left,
        )

    def k_copy(up, d, h):
        origin = gy - (d - 1) if up else gy + (d - 1)
        place = pl.ds(jnp.clip(origin, 0, n_gy - 1) * own_slots, own_slots)
        piece = pl.ds(h * (nb // HALVES), nb // HALVES)
        side = 1 if up else 0
        return remote(
            packs.at[place, piece], packs.at[place, piece],
            k_send.at[side, d - 1, h], k_recv.at[side, d - 1, h], gy=beside(side),
        )

    def k_sends(d, h, action):
        pl.when((gy - (d - 1) >= 0) & has_high)(lambda: action(k_copy(True, d, h)))
        pl.when((gy + (d - 1) < n_gy) & has_low)(lambda: action(k_copy(False, d, h)))

    def k_arrived(d, h):
        pl.when(gy - d >= 0)(lambda: k_copy(True, d, h).wait_recv())
        pl.when(gy + d < n_gy)(lambda: k_copy(False, d, h).wait_recv())

    def k_relay(d):
        for h in range(HALVES):
            k_arrived(d - 1, h)
            k_sends(d, h, lambda copy: copy.start())

    def edge_copy(side, group, index):
        y = 0 if side == 0 else rows_y - 1
        return remote(
            phi.at[y, group_at(group)], edges.at[1 - side, group_at(group)],
            e_send.at[side, index], e_recv.at[1 - side, index], gy=beside(side),
        )

    def edges_arrived(group, index):
        both_sides(lambda side: edge_copy(1 - side, group, index).wait_recv())

    def share_copy(side):
        return remote(
            edges.at[side, group_at(1)], edges.at[side, group_at(far)],
            f_send.at[side], f_recv.at[side], gx=partner,
        )

    def apply_rows(group, chosen):
        for i in range(nb):
            p = group * nb + i
            line = {-1: edges[0, p], rows_y: edges[1, p]} if chosen == outer else {}
            for y in range(rows_y):
                line[y] = phi[y, p]
            line = {y: value.astype(f32) for y, value in line.items()}
            for y in chosen:
                center = line[y]
                around = (
                    line[y + 1] + line[y - 1] + pltpu.roll(center, 1, 1) + pltpu.roll(center, depth - 1, 1)
                )
                applied = -0.5 * (around - 4.0 * center) + pot_ref[y : y + 1, :] * center
                app[y, p] = applied.astype(bf16)

    def picks(a):
        start = nb * n_gx + nb - nb * gx
        found = [lax.rem(cols_ref[k, a] + start, nb * n_gx) for k in range(slots)]
        return [jnp.minimum(p, 3 * nb - 1) for p in found]

    def halo_copy(side, i, c):
        y = i if side == 0 else rows_y - SWEEPS + i
        piece = pl.ds(c * CHUNK, CHUNK)
        return remote(
            halo_out.at[y, piece], halo_in.at[1 - side, i, piece],
            g_send.at[side, i, c], g_recv.at[1 - side, i, c], gy=beside(side),
        )

    def gradient_of(chosen):
        for a in range(nb):
            where = picks(a)
            mixing = jnp.concatenate([packs[k, a] for k in range(slots)], axis=1)
            source = jnp.concatenate(
                [
                    jnp.concatenate([v for p in where for v in (app[y, p], phi[y, p])], axis=0)
                    for y in chosen
                ],
                axis=1,
            )
            total = jnp.dot(mixing, source, preferred_element_type=f32)
            for j, y in enumerate(chosen):
                piece = total[:, j * depth : (j + 1) * depth]
                grad[a, y] = piece
                halo_out[y, a] = piece.astype(bf16)
            if a % CHUNK == CHUNK - 1:
                for y in chosen:
                    if y < SWEEPS:
                        pl.when(has_low)(lambda: halo_copy(0, y, a // CHUNK).start())
                    if y >= rows_y - SWEEPS:
                        pl.when(has_high)(
                            lambda: halo_copy(1, y - rows_y + SWEEPS, a // CHUNK).start()
                        )

    def part_of(a):
        def whole(block, p):
            return jnp.concatenate([block[y, p] for y in range(rows_y)], axis=1)

        source = jnp.concatenate([whole(app, p) for p in picks(a)], axis=0)
        block = lax.dot_general(
            whole(phi, nb + a), source, (((1,), (1,)), ((), ())), preferred_element_type=f32
        ) * volume
        for k in range(slots):
            one = block[:, k * size : (k + 1) * size]
            part[k, a] = jnp.concatenate([one[:half], one[half:]], axis=1)

    def split(value):
        return [value[i : i + 8] for i in range(0, half, 8)]

    def encode(s):
        for j in range(own_slots):
            spot = s * own_slots + j
            top = jnp.full((8, 2 * size), 1e-33, f32)
            for a in range(nb):
                for value in split(part[spot, a]):
                    top = jnp.maximum(top, jnp.abs(value))
            top_out[spot] = top
            scale = TOP / top
            for a in range(nb):
                coded = jnp.concatenate([value * scale for value in split(part[spot, a])], axis=0)
                code_out[spot, a] = jnp.round(coded).astype(jnp.int32).astype(jnp.int16)

    def decoded(off, j, a):
        step = top_in[off - 1, j] * (1.0 / TOP)
        coded = code_in[off - 1, j, a].astype(jnp.int32).astype(f32)
        return jnp.concatenate([value * step for value in split(coded)], axis=0)

    def part_copies(off):
        peer = lax.rem(gy + off, n_gy)
        place = pl.ds(peer * own_slots, own_slots)
        return (
            remote(
                top_out.at[place], top_in.at[off - 1], t_send.at[off - 1], t_recv.at[off - 1], gy=peer
            ),
            remote(
                code_out.at[place], code_in.at[off - 1], h_send.at[off - 1], h_recv.at[off - 1], gy=peer
            ),
        )

    def pass_on(off):
        encode(lax.rem(gy + off, n_gy))
        for copy in part_copies(off):
            copy.start()

    diag = 1.0 + 2.0 / kinetic_cut
    coef = 0.5 / kinetic_cut
    low, high = jnp.where(has_low, 1.0, 0.0).astype(f32), jnp.where(has_high, 1.0, 0.0).astype(f32)
    z_index = lax.broadcasted_iota(jnp.int32, (size, depth), 1)

    def finish(a):
        field = [halo_in[0, i, a].astype(f32) for i in range(SWEEPS)]
        field += [grad[a, y] for y in range(rows_y)]
        field += [halo_in[1, i, a].astype(f32) for i in range(SWEEPS)]
        field = [value * (1.0 / diag) for value in field]
        now = list(field)
        for sweep in range(1, SWEEPS + 1):
            later = list(now)
            for i in range(sweep, rows_y + 2 * SWEEPS - sweep):
                around = now[i - 1] + now[i + 1]
                around = around + pltpu.roll(now[i], 1, 1) + pltpu.roll(now[i], depth - 1, 1)
                value = field[i] + (coef / diag) * around
                if i < SWEEPS:
                    value = value * low
                if i >= rows_y + SWEEPS:
                    value = value * high
                later[i] = value
            now = later
        z_in = (z_index >= regs_ref[2, a]) & (z_index < regs_ref[3, a])
        for y in range(rows_y):
            spot = gy * rows_y + y
            y_in = jnp.where((spot >= regs_ref[0, a]) & (spot < regs_ref[1, a]), step_length, 0.0)
            masked = jnp.where(z_in, now[SWEEPS + y] * y_in.astype(f32), 0.0)
            out_ref[pl.ds(a * brick + y, size, stride=rows_y), :] = phi[y, nb + a].astype(f32) - masked

    loads[0].wait()
    wide[...] = x_ref[...].astype(f32)
    for y in outer + inner:
        for a in range(nb):
            phi[y, nb + a] = wide[pl.ds(a * brick + y, size, stride=rows_y), :].astype(bf16)
    loads[1].wait()
    loads[2].wait()
    for j in range(own_slots):
        for a in range(nb):
            packs[gy * own_slots + j, a] = jnp.concatenate([kern_ref[j, a], -wght_ref[j, a]], axis=1)

    pl.semaphore_wait(barrier, 2 + has_low.astype(jnp.int32) + has_high.astype(jnp.int32))
    for y in outer + inner:
        x_copy(0, y).start()
        x_copy(2, y).start()
    for h in range(HALVES):
        k_sends(1, h, lambda copy: copy.start())
    for load in loads[3:]:
        load.wait()
    apply_rows(1, inner)
    if n_gy > 2:
        k_relay(2)
    both_sides(lambda side: edge_copy(side, 1, 0).start())
    for y in range(rows_y):
        x_copy(near, y).wait_recv()
    apply_rows(near, inner)
    for d in range(3, n_gy):
        k_relay(d)
    x_copy(far, outer[0]).wait_recv()
    pl.when(has_low)(lambda: edge_copy(0, far, 1).start())
    x_copy(far, outer[1]).wait_recv()
    pl.when(has_high)(lambda: edge_copy(1, far, 1).start())
    edges_arrived(1, 0)
    both_sides(lambda side: share_copy(side).start())
    apply_rows(1, outer)
    for y in inner:
        x_copy(far, y).wait_recv()
    apply_rows(far, inner)
    for h in range(HALVES):
        k_arrived(n_gy - 1, h)
    gradient_of(inner)
    both_sides(lambda side: share_copy(side).wait_recv())
    apply_rows(near, outer)
    edges_arrived(far, 1)
    apply_rows(far, outer)
    gradient_of(outer)
    for a in range(nb):
        part_of(a)
    for off in range(1, n_gy):
        pass_on(off)
    for c in range(chunks):
        for i in range(SWEEPS):
            both_sides(lambda side: halo_copy(1 - side, i, c).wait_recv())
        for a in range(c * CHUNK, (c + 1) * CHUNK):
            finish(a)

    def take(off):
        for copy in part_copies(off):
            copy.wait_recv()
        for j in range(own_slots):
            for a in range(nb):
                mine = gy * own_slots + j
                part[mine, a] = part[mine, a] + decoded(off, j, a)

    for off in range(1, n_gy):
        take(off)
    for j in range(own_slots):
        for a in range(nb):
            total = part[gy * own_slots + j, a]
            ham_ref[j, a, :half, :] = total[:, :size]
            ham_ref[j, a, half:, :] = total[:, size:]

    for y in range(rows_y):
        x_copy(0, y).wait_send()
        x_copy(2, y).wait_send()
    both_sides(lambda side: share_copy(side).wait_send())
    both_sides(lambda side: edge_copy(side, 1, 0).wait_send())
    both_sides(lambda side: edge_copy(side, far, 1).wait_send())
    for d in range(1, n_gy):
        for h in range(HALVES):
            k_sends(d, h, lambda copy: copy.wait_send())
    for c in range(chunks):
        for i in range(SWEEPS):
            both_sides(lambda side: halo_copy(side, i, c).wait_send())

    for off in range(1, n_gy):
        for copy in part_copies(off):
            copy.wait_send()


def store_body(support_ref, ham_ref, support_out, ham_out, sem):
    copies = [
        pltpu.make_async_copy(support_ref, support_out, sem.at[0]),
        pltpu.make_async_copy(ham_ref, ham_out, sem.at[1]),
    ]
    for copy in copies:
        copy.start()
    for copy in copies:
        copy.wait()


def local(n_gx, n_gy, support_funcs, potential, kernel, weighted, columns, regions):
    own_slots, nb, size = kernel.shape[:3]
    orbitals, rows_y, depth = support_funcs.shape
    slots = own_slots * n_gy
    flat = orbitals * rows_y
    chunks = nb // CHUNK
    vmem = pl.BlockSpec(memory_space=pltpu.VMEM)
    dma = pltpu.SemaphoreType.DMA
    operands = (
        columns.T, regions.T, potential, support_funcs.reshape(flat, depth), kernel, weighted
    )
    planes = (rows_y, 3 * nb, size, depth)
    parts = (slots, nb, size // 2, 2 * size)
    new_support, hamiltonian = pl.pallas_call(
        functools.partial(kernel_body, n_gx, n_gy, rows_y),
        out_shape=(
            jax.ShapeDtypeStruct((flat, depth), f32),
            jax.ShapeDtypeStruct((own_slots, nb, size, size), f32),
        ),
        in_specs=[pl.BlockSpec(memory_space=pltpu.HBM)] * 6,
        out_specs=(vmem, vmem),
        scratch_shapes=[
            pltpu.SMEM((slots, nb), jnp.int32),
            pltpu.SMEM((4, nb), jnp.int32),
            pltpu.VMEM((rows_y, depth), f32),
            pltpu.VMEM((flat, depth), bf16),
            pltpu.VMEM(kernel.shape, bf16),
            pltpu.VMEM(kernel.shape, bf16),
            pltpu.VMEM((flat, depth), f32),
            pltpu.VMEM(planes, bf16),
            pltpu.VMEM(planes, bf16),
            pltpu.VMEM((2, 3 * nb, size, depth), bf16),
            pltpu.VMEM((slots, nb, size, 2 * size), bf16),
            pltpu.VMEM((nb, rows_y, size, depth), f32),
            pltpu.VMEM((rows_y, nb, size, depth), bf16),
            pltpu.VMEM((2, SWEEPS, nb, size, depth), bf16),
            pltpu.VMEM(parts, f32),
            pltpu.VMEM(parts, jnp.int16),
            pltpu.VMEM((n_gy - 1, own_slots) + parts[1:], jnp.int16),
            pltpu.VMEM((slots, 8, 2 * size), f32),
            pltpu.VMEM((n_gy - 1, own_slots, 8, 2 * size), f32),
            dma((6,)),
            dma((3, rows_y)),
            dma((3, rows_y)),
            dma((2, 2)),
            dma((2, 2)),
            dma((2,)),
            dma((2,)),
            dma((2, n_gy - 1, HALVES)),
            dma((2, n_gy - 1, HALVES)),
            dma((2, SWEEPS, chunks)),
            dma((2, SWEEPS, chunks)),
            dma((n_gy - 1,)),
            dma((n_gy - 1,)),
            dma((n_gy - 1,)),
            dma((n_gy - 1,)),
        ],
        compiler_params=pltpu.CompilerParams(
            collective_id=0, has_side_effects=True, vmem_limit_bytes=40 * 1024 * 1024
        ),
    )(*[pltpu.with_memory_space_constraint(v, pltpu.HBM) for v in operands])
    hbm = pl.BlockSpec(memory_space=pltpu.HBM)
    new_support, hamiltonian = pl.pallas_call(
        store_body,
        out_shape=(
            jax.ShapeDtypeStruct(new_support.shape, f32),
            jax.ShapeDtypeStruct(hamiltonian.shape, f32),
        ),
        in_specs=[vmem, vmem],
        out_specs=(hbm, hbm),
        scratch_shapes=[dma((2,))],
        compiler_params=pltpu.CompilerParams(vmem_limit_bytes=8 * 1024 * 1024),
    )(new_support, hamiltonian)
    return (new_support.reshape(orbitals, rows_y, depth), hamiltonian)


def solution(mesh):
    return jax.shard_map(
        functools.partial(local, mesh.shape["gx"], mesh.shape["gy"]),
        mesh=mesh,
        in_specs=(
            P("gx", "gy", None),
            P("gy", None),
            P("gy", "gx", None, None),
            P("gy", "gx", None, None),
            P("gx", None),
            P("gx", None),
        ),
        out_specs=(P("gx", "gy", None), P("gy", "gx", None, None)),
        check_vma=False,
    )
```

time: 34.2 us -> 30.5 us (0.89)
  Pallas kernels: 33.4 us -> 29.7 us
    pallas_call x1, Pallas kernels: 32.4 us -> 28.8 us  [local(): pl.pallas_call(functools.partial(kernel_body, n_gx, n_gy, rows_y), out_sh...]
where the time goes in v1:
time: 30.5 us; the launch traced here: 30.4 us
  Pallas kernels  29.7 us (97%)
  between operations  0.64 us (2%)
    pallas_call x1, Pallas kernels, local(): pl.pallas_call(functools.partial(kernel_body, n_gx, n_gy, rows_y), out_sh...  28.8 us
    pallas_call x1, Pallas kernels, local(): pl.pallas_call(store_body, out_shape=(jax.ShapeDtypeStruct(new_support.sh...  0.96 us

profile of v1, /device:TPU:0, one launch (start us, length us, event | category | flops | bytes accessed | tf_op | source)
XLA Modules:
  0.0 30.4 jit_solution(18211391732055255273)
XLA Ops:
  0.6 28.8 %shard_map.77 = (f32[1536,128]{1,0:T(8,128)S(1)}, f32[1,6,64,64]{3,2,1,0:T(8,128)S(1)}) custom-call(s32[4,6]{1,0:T(4,128)} %bitcast.5, s32[4,6]{1,0:T(4,128)} %bitcast.6, f32[4,128]{1,0:T(4,128)} %pot_hbm.1, bf16[1536,128]{1,0:T(8,128)(2,1)} %bitcast.4, bf16[1,6,64,64]{3,2,1,0:T(8,128)(2,1)} %kern_hbm.1, bf16[1,6,64,64]{3,2,1,0:T(8,128)(2,1)} %wght_hbm.1), custom_call_target="tpu_custom_call" | custom-call | tf_op jit(solution)/shard_map/pallas_call | solution.py:385
  29.4 1.0 %shard_map.78 = (f32[1536,128]{1,0:T(8,128)}, f32[1,6,64,64]{3,2,1,0:T(8,128)}) custom-call(f32[1536,128]{1,0:T(8,128)S(1)} %get-tuple-element.6.support_ref, f32[1,6,64,64]{3,2,1,0:T(8,128)S(1)} %get-tuple-element.7.ham_ref), custom_call_target="tpu_custom_call" | custom-call | tf_op jit(solution)/shard_map/pallas_call | solution.py:434

commit v2 on v1

--- a/solution.py
+++ b/solution.py
@@ -39,14 +39,15 @@
     cols_ref, regs_ref, pot_ref, x_ref, kern_ref, wght_ref, wide, phi, app, edges, packs,
     grad, halo_out, halo_in, part, code_out, code_in, top_out, top_in, in_sem,
     x_send, x_recv, e_send, e_recv, f_send, f_recv, k_send, k_recv, g_send, g_recv,
-    h_send, h_recv, t_send, t_recv,
+    h_send, h_recv, t_send, t_recv, a_send, a_recv,
 ):
     gx, gy = lax.axis_index("gx"), lax.axis_index("gy")
     right, left = lax.rem(gx + 1, n_gx), lax.rem(gx + n_gx - 1, n_gx)
-    partner = gx + 1 - 2 * lax.rem(gx, 2)
+    odd = lax.rem(gx, 2)
+    partner, outside = gx + 1 - 2 * odd, jnp.where(odd == 1, right, left)
     above, below = jnp.minimum(gy + 1, n_gy - 1), jnp.maximum(gy - 1, 0)
     has_low, has_high = gy > 0, gy < n_gy - 1
-    near = 2 - 2 * lax.rem(gx, 2)
+    near = 2 - 2 * odd
     far = 2 - near
     own_slots, nb, size = kern_ref.shape[:3]
     slots = own_slots * n_gy
@@ -58,7 +59,7 @@
     inner, outer = tuple(range(1, rows_y - 1)), (0, rows_y - 1)
 
     pairs = (
-        (x_hbm, x_ref), (kern_hbm, kern_ref), (wght_hbm, wght_ref),
+        (kern_hbm, kern_ref), (wght_hbm, wght_ref), (x_hbm, x_ref),
         (pot_hbm, pot_ref), (cols_hbm, cols_ref), (regs_hbm, regs_ref),
     )
     loads = [pltpu.make_async_copy(src, dst, in_sem.at[i]) for i, (src, dst) in enumerate(pairs)]
@@ -92,7 +93,7 @@
 
     def x_copy(group, y):
         return remote(
-            phi.at[y, group_at(1)], phi.at[y, group_at(group)],
+            phi[y].at[group_at(1)], phi[y].at[group_at(group)],
             x_send.at[group, y], x_recv.at[group, y], gx=right if isinstance(group, int) and group == 0 else left,
         )
 
@@ -122,7 +123,7 @@
     def edge_copy(side, group, index):
         y = 0 if side == 0 else rows_y - 1
         return remote(
-            phi.at[y, group_at(group)], edges.at[1 - side, group_at(group)],
+            phi[y].at[group_at(group)], edges.at[1 - side, group_at(group)],
             e_send.at[side, index], e_recv.at[1 - side, index], gy=beside(side),
         )
 
@@ -134,21 +135,37 @@
             edges.at[side, group_at(1)], edges.at[side, group_at(far)],
             f_send.at[side], f_recv.at[side], gx=partner,
         )
+
+    def across_copy(side):
+        return remote(
+            edges.at[side, group_at(1)], edges.at[side, group_at(near)],
+            a_send.at[side], a_recv.at[side], gx=outside,
+        )
+
+    def across(action):
+        pl.when(gy == 0)(lambda: action(1))
+        pl.when(gy > 0)(lambda: action(0))
+
+    def across_arrived(side):
+        remote(
+            edges.at[side, group_at(1)], edges.at[side, group_at(far)],
+            a_send.at[side], a_recv.at[side], gx=outside,
+        ).wait_recv()
 
     def apply_rows(group, chosen):
         for i in range(nb):
             p = group * nb + i
-            line = {-1: edges[0, p], rows_y: edges[1, p]} if chosen == outer else {}
-            for y in range(rows_y):
-                line[y] = phi[y, p]
-            line = {y: value.astype(f32) for y, value in line.items()}
+            line = {}
+            for y in sorted({y + step for y in chosen for step in (-1, 0, 1)}):
+                inside = phi[y][p] if 0 <= y < rows_y else edges[0 if y < 0 else 1, p]
+                line[y] = inside.astype(f32)
             for y in chosen:
                 center = line[y]
                 around = (
                     line[y + 1] + line[y - 1] + pltpu.roll(center, 1, 1) + pltpu.roll(center, depth - 1, 1)
                 )
                 applied = -0.5 * (around - 4.0 * center) + pot_ref[y : y + 1, :] * center
-                app[y, p] = applied.astype(bf16)
+                app[y][p] = applied.astype(bf16)
 
     def picks(a):
         start = nb * n_gx + nb - nb * gx
@@ -169,7 +186,7 @@
             mixing = jnp.concatenate([packs[k, a] for k in range(slots)], axis=1)
             source = jnp.concatenate(
                 [
-                    jnp.concatenate([v for p in where for v in (app[y, p], phi[y, p])], axis=0)
+                    jnp.concatenate([v for p in where for v in (app[y][p], phi[y][p])], axis=0)
                     for y in chosen
                 ],
                 axis=1,
@@ -190,7 +207,7 @@
 
     def part_of(a):
         def whole(block, p):
-            return jnp.concatenate([block[y, p] for y in range(rows_y)], axis=1)
+            return jnp.concatenate([block[y][p] for y in range(rows_y)], axis=1)
 
         source = jnp.concatenate([whole(app, p) for p in picks(a)], axis=0)
         block = lax.dot_general(
@@ -266,58 +283,62 @@
             spot = gy * rows_y + y
             y_in = jnp.where((spot >= regs_ref[0, a]) & (spot < regs_ref[1, a]), step_length, 0.0)
             masked = jnp.where(z_in, now[SWEEPS + y] * y_in.astype(f32), 0.0)
-            out_ref[pl.ds(a * brick + y, size, stride=rows_y), :] = phi[y, nb + a].astype(f32) - masked
+            out_ref[pl.ds(a * brick + y, size, stride=rows_y), :] = phi[y][nb + a].astype(f32) - masked
 
     loads[0].wait()
-    wide[...] = x_ref[...].astype(f32)
-    for y in outer + inner:
-        for a in range(nb):
-            phi[y, nb + a] = wide[pl.ds(a * brick + y, size, stride=rows_y), :].astype(bf16)
     loads[1].wait()
-    loads[2].wait()
     for j in range(own_slots):
         for a in range(nb):
             packs[gy * own_slots + j, a] = jnp.concatenate([kern_ref[j, a], -wght_ref[j, a]], axis=1)
+    loads[2].wait()
+    wide[...] = x_ref[...].astype(f32)
 
     pl.semaphore_wait(barrier, 2 + has_low.astype(jnp.int32) + has_high.astype(jnp.int32))
-    for y in outer + inner:
+    for h in range(HALVES):
+        k_sends(1, h, lambda copy: copy.start())
+    for y in range(rows_y):
+        for a in range(nb):
+            phi[y][nb + a] = wide[pl.ds(a * brick + y, size, stride=rows_y), :].astype(bf16)
         x_copy(0, y).start()
         x_copy(2, y).start()
-    for h in range(HALVES):
-        k_sends(1, h, lambda copy: copy.start())
+    both_sides(lambda side: edge_copy(side, 1, 0).start())
     for load in loads[3:]:
         load.wait()
     apply_rows(1, inner)
     if n_gy > 2:
         k_relay(2)
-    both_sides(lambda side: edge_copy(side, 1, 0).start())
     for y in range(rows_y):
         x_copy(near, y).wait_recv()
     apply_rows(near, inner)
+    x_copy(far, 0).wait_recv()
+    pl.when(gy > 1)(lambda: edge_copy(0, far, 1).start())
     for d in range(3, n_gy):
         k_relay(d)
-    x_copy(far, outer[0]).wait_recv()
-    pl.when(has_low)(lambda: edge_copy(0, far, 1).start())
-    x_copy(far, outer[1]).wait_recv()
-    pl.when(has_high)(lambda: edge_copy(1, far, 1).start())
     edges_arrived(1, 0)
+    across(lambda side: across_copy(side).start())
     both_sides(lambda side: share_copy(side).start())
     apply_rows(1, outer)
-    for y in inner:
-        x_copy(far, y).wait_recv()
-    apply_rows(far, inner)
-    for h in range(HALVES):
-        k_arrived(n_gy - 1, h)
-    gradient_of(inner)
     both_sides(lambda side: share_copy(side).wait_recv())
     apply_rows(near, outer)
-    edges_arrived(far, 1)
-    apply_rows(far, outer)
-    gradient_of(outer)
+    x_copy(far, 1).wait_recv()
+    for y in inner:
+        x_copy(far, y + 1).wait_recv()
+        apply_rows(far, (y,))
+        if y == inner[0]:
+            for h in range(HALVES):
+                k_arrived(n_gy - 1, h)
+        gradient_of((y,))
+    pl.when(gy == 0)(lambda: across_arrived(1))
+    pl.when((gy > 0) & has_high)(lambda: edge_copy(0, far, 1).wait_recv())
+    apply_rows(far, outer[1:])
+    gradient_of(outer[1:])
+    pl.when(gy > 0)(lambda: across_arrived(0))
+    apply_rows(far, outer[:1])
     for a in range(nb):
         part_of(a)
-    for off in range(1, n_gy):
-        pass_on(off)
+    gradient_of(outer[:1])
+    for i in range(1, n_gy):
+        pass_on(jnp.where(gy < n_gy // 2, n_gy - i, i))
     for c in range(chunks):
         for i in range(SWEEPS):
             both_sides(lambda side: halo_copy(1 - side, i, c).wait_recv())
@@ -345,7 +366,8 @@
         x_copy(2, y).wait_send()
     both_sides(lambda side: share_copy(side).wait_send())
     both_sides(lambda side: edge_copy(side, 1, 0).wait_send())
-    both_sides(lambda side: edge_copy(side, far, 1).wait_send())
+    pl.when(gy > 1)(lambda: edge_copy(0, far, 1).wait_send())
+    across(lambda side: across_copy(side).wait_send())
     for d in range(1, n_gy):
         for h in range(HALVES):
             k_sends(d, h, lambda copy: copy.wait_send())
@@ -380,7 +402,7 @@
     operands = (
         columns.T, regions.T, potential, support_funcs.reshape(flat, depth), kernel, weighted
     )
-    planes = (rows_y, 3 * nb, size, depth)
+    planes = [pltpu.VMEM((3 * nb, size, depth), bf16) for _ in range(rows_y)]
     parts = (slots, nb, size // 2, 2 * size)
     new_support, hamiltonian = pl.pallas_call(
         functools.partial(kernel_body, n_gx, n_gy, rows_y),
@@ -398,8 +420,8 @@
             pltpu.VMEM(kernel.shape, bf16),
             pltpu.VMEM(kernel.shape, bf16),
             pltpu.VMEM((flat, depth), f32),
-            pltpu.VMEM(planes, bf16),
-            pltpu.VMEM(planes, bf16),
+            planes,
+            planes,
             pltpu.VMEM((2, 3 * nb, size, depth), bf16),
             pltpu.VMEM((slots, nb, size, 2 * size), bf16),
             pltpu.VMEM((nb, rows_y, size, depth), f32),
@@ -425,6 +447,8 @@
             dma((n_gy - 1,)),
             dma((n_gy - 1,)),
             dma((n_gy - 1,)),
+            dma((2,)),
+            dma((2,)),
         ],
         compiler_params=pltpu.CompilerParams(
             collective_id=0, has_side_effects=True, vmem_limit_bytes=40 * 1024 * 1024

time: 30.5 us -> 29.1 us (0.954)
  Pallas kernels: 29.7 us -> 28.3 us
    pallas_call x1, Pallas kernels: 28.8 us -> 27.4 us  [local(): pl.pallas_call(functools.partial(kernel_body, n_gx, n_gy, rows_y), out_sh...]
where the time goes in v2:
time: 29.1 us; the launch traced here: 29 us
  Pallas kernels  28.3 us (97%)
  between operations  0.64 us (2%)
    pallas_call x1, Pallas kernels, local(): pl.pallas_call(functools.partial(kernel_body, n_gx, n_gy, rows_y), out_sh...  27.4 us
    pallas_call x1, Pallas kernels, local(): pl.pallas_call(store_body, out_shape=(jax.ShapeDtypeStruct(new_support.sh...  0.96 us

profile of v2, /device:TPU:0, one launch (start us, length us, event | category | flops | bytes accessed | tf_op | source)
XLA Modules:
  0.0 29.0 jit_solution(3313484026567582758)
XLA Ops:
  0.6 27.4 %shard_map.77 = (f32[1536,128]{1,0:T(8,128)S(1)}, f32[1,6,64,64]{3,2,1,0:T(8,128)S(1)}) custom-call(s32[4,6]{1,0:T(4,128)} %bitcast.5, s32[4,6]{1,0:T(4,128)} %bitcast.6, f32[4,128]{1,0:T(4,128)} %pot_hbm.1, bf16[1536,128]{1,0:T(8,128)(2,1)} %bitcast.4, bf16[1,6,64,64]{3,2,1,0:T(8,128)(2,1)} %kern_hbm.1, bf16[1,6,64,64]{3,2,1,0:T(8,128)(2,1)} %wght_hbm.1), custom_call_target="tpu_custom_call" | custom-call | tf_op jit(solution)/shard_map/pallas_call | solution.py:407
  28.0 1.0 %shard_map.78 = (f32[1536,128]{1,0:T(8,128)}, f32[1,6,64,64]{3,2,1,0:T(8,128)}) custom-call(f32[1536,128]{1,0:T(8,128)S(1)} %get-tuple-element.6.support_ref, f32[1,6,64,64]{3,2,1,0:T(8,128)S(1)} %get-tuple-element.7.ham_ref), custom_call_target="tpu_custom_call" | custom-call | tf_op jit(solution)/shard_map/pallas_call | solution.py:458

commit v3 on v2

--- a/solution.py
+++ b/solution.py
@@ -8,7 +8,7 @@
 from jax.sharding import PartitionSpec as P
 
 SWEEPS = 3
-CHUNK = 2
+CHUNK = 3
 HALVES = 2
 TOP = 32767.0
 kinetic_cut = 1.0
@@ -314,12 +314,6 @@
     pl.when(gy > 1)(lambda: edge_copy(0, far, 1).start())
     for d in range(3, n_gy):
         k_relay(d)
-    edges_arrived(1, 0)
-    across(lambda side: across_copy(side).start())
-    both_sides(lambda side: share_copy(side).start())
-    apply_rows(1, outer)
-    both_sides(lambda side: share_copy(side).wait_recv())
-    apply_rows(near, outer)
     x_copy(far, 1).wait_recv()
     for y in inner:
         x_copy(far, y + 1).wait_recv()
@@ -328,6 +322,13 @@
             for h in range(HALVES):
                 k_arrived(n_gy - 1, h)
         gradient_of((y,))
+        if y == inner[0]:
+            edges_arrived(1, 0)
+            across(lambda side: across_copy(side).start())
+            both_sides(lambda side: share_copy(side).start())
+            apply_rows(1, outer)
+    both_sides(lambda side: share_copy(side).wait_recv())
+    apply_rows(near, outer)
     pl.when(gy == 0)(lambda: across_arrived(1))
     pl.when((gy > 0) & has_high)(lambda: edge_copy(0, far, 1).wait_recv())
     apply_rows(far, outer[1:])

time: 29.1 us -> 28.7 us (0.986)
  the two profiles are of different devices: /device:TPU:0 before, /device:TPU:1 now
where the time goes in v3:
time: 28.7 us; the launch traced here: 28.6 us
  Pallas kernels  28 us (98%)
  between operations  0.64 us (2%)
    pallas_call x1, Pallas kernels, local(): pl.pallas_call(functools.partial(kernel_body, n_gx, n_gy, rows_y), out_sh...  27 us
    pallas_call x1, Pallas kernels, local(): pl.pallas_call(store_body, out_shape=(jax.ShapeDtypeStruct(new_support.sh...  0.96 us

profile of v3, /device:TPU:1, one launch (start us, length us, event | category | flops | bytes accessed | tf_op | source)
XLA Modules:
  0.0 28.6 jit_solution(8805645934753654374)
XLA Ops:
  0.6 27.0 %shard_map.77 = (f32[1536,128]{1,0:T(8,128)S(1)}, f32[1,6,64,64]{3,2,1,0:T(8,128)S(1)}) custom-call(s32[4,6]{1,0:T(4,128)} %bitcast.5, s32[4,6]{1,0:T(4,128)} %bitcast.6, f32[4,128]{1,0:T(4,128)} %pot_hbm.1, bf16[1536,128]{1,0:T(8,128)(2,1)} %bitcast.4, bf16[1,6,64,64]{3,2,1,0:T(8,128)(2,1)} %kern_hbm.1, bf16[1,6,64,64]{3,2,1,0:T(8,128)(2,1)} %wght_hbm.1), custom_call_target="tpu_custom_call" | custom-call | tf_op jit(solution)/shard_map/pallas_call | solution.py:408
  27.6 1.0 %shard_map.78 = (f32[1536,128]{1,0:T(8,128)}, f32[1,6,64,64]{3,2,1,0:T(8,128)}) custom-call(f32[1536,128]{1,0:T(8,128)S(1)} %get-tuple-element.6.support_ref, f32[1,6,64,64]{3,2,1,0:T(8,128)S(1)} %get-tuple-element.7.ham_ref), custom_call_target="tpu_custom_call" | custom-call | tf_op jit(solution)/shard_map/pallas_call | solution.py:459
